TPU v7x, 32 devices: a whole 2x2x4 slice. The times are simulated.
32 devices in a mesh: blk: 2 (over y), uly: 16 (over z, x, core).
Axes of the slice: x: 2, y: 2, z: 4, core: 2. Of those that a mesh axis runs over, the one named last changes fastest.
Arguments:
- queries: bfloat16 [4096, 2048], P(('blk', 'uly')), may hold values from -8 to 8
- keys: bfloat16 [4096, 2048], P(('blk', 'uly')), may hold values from -8 to 8
- values: bfloat16 [4096, 2048], P(('blk', 'uly')), may hold values from -6 to 6
- grad_out: bfloat16 [4096, 2048], P(('blk', 'uly')), may hold values from -6 to 6
- doc_start: int32 [32], replicated, may hold values from 0 to 3968, as said below
Outputs:
- grad_queries: bfloat16 [4096, 2048], P(('blk', 'uly'))
- grad_keys: bfloat16 [4096, 2048], P(('blk', 'uly'))
- grad_values: bfloat16 [4096, 2048], P(('blk', 'uly'))
Inputs may be any that keep to these rules, and one draw needn't show every extreme that they name: `doc_start`: each entry is the first position of its block's document, so documents are runs of whole blocks; no document is longer than 8 blocks and one is exactly 8; a document crosses every boundary between groups of 2048 positions and starts at most 7 blocks before it, at one boundary exactly 7; the last block starts a document.
All inputs are finite; a program needn't handle non-finite values.
Results may differ from a plain program's by a relative error of at most 0.0051.
Values may be sent and summed in bfloat16 or wider, within the bound.
A program may use at most 64 MiB of HBM per device.

v0:
```python
import functools
import math

import jax
import jax.numpy as jnp
from jax import lax
from jax.experimental import pallas as pl
from jax.experimental.pallas import tpu as pltpu
from jax.sharding import PartitionSpec as P

MAXB = 8
MESH = pl.DeviceIdType.MESH


def nt_dot(a, b):
    return lax.dot_general(a, b, (((1,), (1,)), ((), ())), preferred_element_type=jnp.float32)


def tn_dot(a, b):
    return lax.dot_general(a, b, (((0,), (0,)), ((), ())), preferred_element_type=jnp.float32)


def nn_dot(a, b):
    return lax.dot_general(a, b, (((1,), (0,)), ((), ())), preferred_element_type=jnp.float32)


def kernel(
    n, groups, rows, width,
    docs, q_in, k_in, v_in, d_in,
    gq, gk, gv,
    ext_k, ext_v, q_all, d_all, dk_acc, dv_acc, dq_low, dk_low, dv_low,
    give_k, give_v, back_k, back_v,
    own_sem, in_send, in_recv, far_send, far_recv, back_send, back_recv,
    out_own, out_send, out_recv,
):
    blk = lax.axis_index("blk")
    me = lax.axis_index("uly")
    reach = MAXB - 1
    far = reach * rows
    tail = far + (n - reach) * rows
    scale = 1.0 / math.sqrt(width)

    barrier = pltpu.get_barrier_semaphore()

    def greet(s, carry):
        pl.semaphore_signal(
            barrier, inc=1, device_id=(blk, lax.rem(me + s, n)), device_id_type=MESH
        )
        return carry

    lax.fori_loop(1, n, greet, 0)

    beside = sorted({1, groups - 1} - {0, groups})
    for by in beside:
        pl.semaphore_signal(
            barrier, inc=1, device_id=(lax.rem(blk + by, groups), me), device_id_type=MESH
        )

    def columns(ref, head):
        return ref.at[:, pl.ds(pl.multiple_of(head * width, width), width)]

    def block(ref, base, index):
        return ref.at[pl.ds(pl.multiple_of(base + index * rows, rows), rows), :]

    streams = ((k_in, ext_k, far), (q_in, q_all, 0), (v_in, ext_v, far), (d_in, d_all, 0))

    own = [
        pltpu.make_async_copy(columns(src, me), block(dst, base, me), own_sem.at[a])
        for a, (src, dst, base) in enumerate(streams)
    ]
    for copy in own:
        copy.start()

    pl.semaphore_wait(barrier, n - 1 + len(beside))

    for a, (src, dst, base) in enumerate(streams):
        def send(s, carry, a=a, src=src, dst=dst, base=base):
            to = lax.rem(me + s, n)
            pltpu.make_async_remote_copy(
                src_ref=columns(src, to),
                dst_ref=block(dst, base, me),
                send_sem=in_send.at[a],
                recv_sem=in_recv.at[a],
                device_id=(blk, to),
                device_id_type=MESH,
            ).start()
            return carry

        lax.fori_loop(1, n, send, 0)

    dk_acc[...] = jnp.zeros_like(dk_acc)
    dv_acc[...] = jnp.zeros_like(dv_acc)

    @pl.when(blk == 0)
    def _():
        ext_k[pl.ds(0, far), :] = jnp.zeros((far, width), ext_k.dtype)
        ext_v[pl.ds(0, far), :] = jnp.zeros((far, width), ext_v.dtype)

    def wait_bytes(sem):
        part = q_all.at[pl.ds(0, (n - 1) * rows), :]
        pltpu.make_async_copy(part, part, sem).wait()

    def forward(ref, a):
        return pltpu.make_async_remote_copy(
            src_ref=ref.at[pl.ds(tail, far), :],
            dst_ref=ref.at[pl.ds(0, far), :],
            send_sem=far_send.at[a],
            recv_sem=far_recv.at[a],
            device_id=(blk + 1, me),
            device_id_type=MESH,
        )

    def arrived(a):
        own[a].wait()
        wait_bytes(in_recv.at[a])

    arrived(0)

    @pl.when(blk < groups - 1)
    def _():
        forward(ext_k, 0).start()

    arrived(1)
    arrived(2)

    @pl.when(blk < groups - 1)
    def _():
        forward(ext_v, 1).start()

    arrived(3)

    @pl.when(blk > 0)
    def _():
        forward(ext_k, 0).wait_recv()
        forward(ext_v, 1).wait_recv()

    window = MAXB * rows
    key_at = lax.broadcasted_iota(jnp.int32, (rows, rows), 0)
    query_at = lax.broadcasted_iota(jnp.int32, (rows, rows), 1)

    def attend(i):
        here = pl.ds(pl.multiple_of(i * rows, rows), rows)
        span = pl.ds(pl.multiple_of(i * rows, rows), window)
        q = q_all[here, :]
        d = d_all[here, :]
        k = ext_k[span, :]
        v = ext_v[span, :]
        score = nt_dot(k, q)
        dprob = nt_dot(v, d)
        mine = blk * n + i
        doc = docs[mine]
        parts = []
        for t in range(reach):
            other = mine - reach + t
            same = (docs[jnp.maximum(other, 0)] == doc) & (other >= 0)
            parts.append(score[t * rows : (t + 1) * rows] + jnp.where(same, 0.0, -1e30))
        parts.append(jnp.where(key_at <= query_at, score[reach * rows :], -1e30))
        score = jnp.concatenate(parts, 0)
        top = jnp.max(score, axis=0, keepdims=True)
        weight = jnp.exp((score - top) * scale)
        share = 1.0 / jnp.sum(weight, axis=0, keepdims=True)
        delta = jnp.sum(weight * dprob, axis=0, keepdims=True) * share
        prob = weight * share
        dscore = (prob * ((dprob - delta) * scale)).astype(jnp.bfloat16)
        dv_acc[span, :] += nn_dot(prob.astype(jnp.bfloat16), d)
        dk_acc[span, :] += nn_dot(dscore, q)
        dq_low[here, :] = tn_dot(dscore, k).astype(jnp.bfloat16)

    def give(src, dst, a, i):
        @pl.when(i != me)
        def _():
            pltpu.make_async_remote_copy(
                src_ref=block(src, 0, i),
                dst_ref=columns(dst, me),
                send_sem=out_send.at[a],
                recv_sem=out_recv.at[a],
                device_id=(blk, i),
                device_id_type=MESH,
            ).start()

    def keep(src, dst, a):
        return pltpu.make_async_copy(block(src, 0, me), columns(dst, me), out_own.at[a])

    def run(first, count):
        def order(s):
            return first + lax.rem(me + s, count)

        def step(s, carry):
            @pl.when(s > 0)
            def _():
                give(dq_low, gq, 0, order(s + count - 1))

            attend(order(s))
            return carry

        lax.fori_loop(0, count, step, 0)
        give(dq_low, gq, 0, order(count - 1))

    run(0, reach)

    def handing(src, dst, a):
        return pltpu.make_async_remote_copy(
            src_ref=src,
            dst_ref=dst,
            send_sem=back_send.at[a],
            recv_sem=back_recv.at[a],
            device_id=(blk - 1, me),
            device_id_type=MESH,
        )

    @pl.when(blk > 0)
    def _():
        give_k[...] = dk_acc[pl.ds(0, far), :].astype(jnp.bfloat16)
        give_v[...] = dv_acc[pl.ds(0, far), :].astype(jnp.bfloat16)
        handing(give_k, back_k, 0).start()
        handing(give_v, back_v, 1).start()

    run(reach, n - reach)

    keep(dq_low, gq, 0).start()

    @pl.when(blk < groups - 1)
    def _():
        handing(give_k, back_k, 0).wait_recv()
        handing(give_v, back_v, 1).wait_recv()
        dk_acc[pl.ds(tail, far), :] += back_k[...].astype(jnp.float32)
        dv_acc[pl.ds(tail, far), :] += back_v[...].astype(jnp.float32)

    dk_low[...] = dk_acc[pl.ds(far, n * rows), :].astype(jnp.bfloat16)
    dv_low[...] = dv_acc[pl.ds(far, n * rows), :].astype(jnp.bfloat16)

    def spread(s, carry):
        to = lax.rem(me + s, n)
        give(dk_low, gk, 1, to)
        give(dv_low, gv, 2, to)
        return carry

    lax.fori_loop(1, n, spread, 0)
    keep(dk_low, gk, 1).start()
    keep(dv_low, gv, 2).start()

    for a, (src, dst) in enumerate(((dq_low, gq), (dk_low, gk), (dv_low, gv))):
        keep(src, dst, a).wait()
        wait_bytes(out_recv.at[a])

    for a in range(4):
        wait_bytes(in_send.at[a])
    for a in range(3):
        wait_bytes(out_send.at[a])

    @pl.when(blk < groups - 1)
    def _():
        forward(ext_k, 0).wait_send()
        forward(ext_v, 1).wait_send()

    @pl.when(blk > 0)
    def _():
        handing(give_k, back_k, 0).wait_send()
        handing(give_v, back_v, 1).wait_send()


def body(n, groups, queries, keys, values, grad_out, doc_start):
    rows, total = queries.shape
    width = total // n
    far = (MAXB - 1) * rows
    low, wide = jnp.bfloat16, jnp.float32
    here = (n * rows, width)
    reach = (far + n * rows, width)
    out = jax.ShapeDtypeStruct((rows, total), low)
    any_space = pl.BlockSpec(memory_space=pl.ANY)
    vmem = pl.BlockSpec(memory_space=pltpu.VMEM)
    dma = pltpu.SemaphoreType.DMA
    return pl.pallas_call(
        functools.partial(kernel, n, groups, rows, width),
        out_shape=(out, out, out),
        in_specs=[pl.BlockSpec(memory_space=pltpu.SMEM)] + [any_space] * 4,
        out_specs=(vmem, vmem, vmem),
        scratch_shapes=[
            pltpu.VMEM(reach, low), pltpu.VMEM(reach, low),
            pltpu.VMEM(here, low), pltpu.VMEM(here, low),
            pltpu.VMEM(reach, wide), pltpu.VMEM(reach, wide),
            pltpu.VMEM(here, low), pltpu.VMEM(here, low), pltpu.VMEM(here, low),
            pltpu.VMEM((far, width), low), pltpu.VMEM((far, width), low),
            pltpu.VMEM((far, width), low), pltpu.VMEM((far, width), low),
            dma((4,)), dma((4,)), dma((4,)), dma((2,)), dma((2,)), dma((2,)), dma((2,)),
            dma((3,)), dma((3,)), dma((3,)),
        ],
        compiler_params=pltpu.CompilerParams(
            collective_id=0, has_side_effects=True, vmem_limit_bytes=48 * 1024 * 1024
        ),
    )(doc_start, queries, keys, values, grad_out)


def solution(mesh):
    split = P(("blk", "uly"), None)
    return jax.shard_map(
        functools.partial(body, mesh.shape["uly"], mesh.shape["blk"]),
        mesh=mesh,
        in_specs=(split, split, split, split, P()),
        out_specs=(split, split, split),
        check_vma=False,
    )
```

profile of v0, /device:TPU:27, one launch (start us, length us, event | category | flops | bytes accessed | tf_op | source)
XLA Modules:
  0.0 101.3 jit_solution(3257674882591805346)
XLA Ops:
  0.6 0.0 copy-start
  0.6 1.0 %copy-done = bf16[128,2048]{1,0:T(8,128)(2,1)S(1)} copy-done((bf16[128,2048]{1,0:T(8,128)(2,1)S(1)}, bf16[128,2048]{1,0:T(8,128)(2,1)}, u32[]{:S(2)}) %copy-start) | copy-done | bytes 524312
  1.7 0.0 copy-start.1
  1.7 1.0 %copy-done.1 = bf16[128,2048]{1,0:T(8,128)(2,1)S(1)} copy-done((bf16[128,2048]{1,0:T(8,128)(2,1)S(1)}, bf16[128,2048]{1,0:T(8,128)(2,1)}, u32[]{:S(2)}) %copy-start.1) | copy-done | bytes 524312
  2.7 0.0 copy-start.2
  2.7 1.0 %copy-done.2 = bf16[128,2048]{1,0:T(8,128)(2,1)S(1)} copy-done((bf16[128,2048]{1,0:T(8,128)(2,1)S(1)}, bf16[128,2048]{1,0:T(8,128)(2,1)}, u32[]{:S(2)}) %copy-start.2) | copy-done | bytes 524312
  3.8 0.0 copy-start.3
  3.8 1.0 %copy-done.3 = bf16[128,2048]{1,0:T(8,128)(2,1)S(1)} copy-done((bf16[128,2048]{1,0:T(8,128)(2,1)S(1)}, bf16[128,2048]{1,0:T(8,128)(2,1)}, u32[]{:S(2)}) %copy-start.3) | copy-done | bytes 524312
  4.8 0.0 copy-start.4
  4.8 0.7 copy-done.4
  5.5 93.4 %shard_map.76 = (bf16[128,2048]{1,0:T(8,128)(2,1)S(1)}, bf16[128,2048]{1,0:T(8,128)(2,1)S(1)}, bf16[128,2048]{1,0:T(8,128)(2,1)S(1)}) custom-call(s32[32]{0:T(128)S(1)} %copy-done.4, bf16[128,2048]{1,0:T(8,128)(2,1)S(1)} %copy-done, bf16[128,2048]{1,0:T(8,128)(2,1)S(1)} %copy-done.1, bf16[128,2048]{1,0:T(8,128)(2,1)S(1)} %copy-done.2, ...), custom_call_target="tpu_custom_call" | custom-call | tf_op jit(solution)/shard_map/pallas_call | solution.py:273
  98.9 0.8 copy.11
  99.7 0.8 copy.12
  100.5 0.8 copy.13
Async XLA Ops:
  0.6 1.0 %copy-start = (bf16[128,2048]{1,0:T(8,128)(2,1)S(1)}, bf16[128,2048]{1,0:T(8,128)(2,1)}, u32[]{:S(2)}) copy-start(bf16[128,2048]{1,0:T(8,128)(2,1)} %q_in.1) | copy-start | bytes 1572868
  1.7 1.0 %copy-start.1 = (bf16[128,2048]{1,0:T(8,128)(2,1)S(1)}, bf16[128,2048]{1,0:T(8,128)(2,1)}, u32[]{:S(2)}) copy-start(bf16[128,2048]{1,0:T(8,128)(2,1)} %k_in.1) | copy-start | bytes 1572868
  2.7 1.0 %copy-start.2 = (bf16[128,2048]{1,0:T(8,128)(2,1)S(1)}, bf16[128,2048]{1,0:T(8,128)(2,1)}, u32[]{:S(2)}) copy-start(bf16[128,2048]{1,0:T(8,128)(2,1)} %v_in.1) | copy-start | bytes 1572868
  3.8 1.0 %copy-start.3 = (bf16[128,2048]{1,0:T(8,128)(2,1)S(1)}, bf16[128,2048]{1,0:T(8,128)(2,1)}, u32[]{:S(2)}) copy-start(bf16[128,2048]{1,0:T(8,128)(2,1)} %d_in.1) | copy-start | bytes 1572868
  4.8 0.7 copy-start.4
where the time goes:
time: 102 us; the launch traced here: 101 us
  Pallas kernels  93.4 us (92%)
  local copies, waits for them, and re-layouts  7.19 us (7%)
    pallas_call x1, Pallas kernels, body(): pl.pallas_call(functools.partial(kernel, n, groups, rows, width), out_sha...  93.4 us
    unnamed x13, local copies, waits for them, and re-layouts  7.19 us

commit v1 on v0

--- a/solution.py
+++ b/solution.py
@@ -26,11 +26,11 @@
 
 def kernel(
     n, groups, rows, width,
-    docs, q_in, k_in, v_in, d_in,
+    docs_in, q_in, k_in, v_in, d_in,
     gq, gk, gv,
-    ext_k, ext_v, q_all, d_all, dk_acc, dv_acc, dq_low, dk_low, dv_low,
+    docs, prob_all, ext_k, ext_v, q_all, d_all, dk_acc, dv_acc, dq_low, dk_low, dv_low,
     give_k, give_v, back_k, back_v,
-    own_sem, in_send, in_recv, far_send, far_recv, back_send, back_recv,
+    docs_sem, own_sem, in_send, in_recv, far_send, far_recv, back_send, back_recv,
     out_own, out_send, out_recv,
 ):
     blk = lax.axis_index("blk")
@@ -41,6 +41,8 @@
     scale = 1.0 / math.sqrt(width)
 
     barrier = pltpu.get_barrier_semaphore()
+    fetch_docs = pltpu.make_async_copy(docs_in, docs, docs_sem)
+    fetch_docs.start()
 
     def greet(s, carry):
         pl.semaphore_signal(
@@ -121,32 +123,20 @@
         forward(ext_k, 0).start()
 
     arrived(1)
-    arrived(2)
-
-    @pl.when(blk < groups - 1)
-    def _():
-        forward(ext_v, 1).start()
-
-    arrived(3)
+    fetch_docs.wait()
 
     @pl.when(blk > 0)
     def _():
         forward(ext_k, 0).wait_recv()
-        forward(ext_v, 1).wait_recv()
 
     window = MAXB * rows
     key_at = lax.broadcasted_iota(jnp.int32, (rows, rows), 0)
     query_at = lax.broadcasted_iota(jnp.int32, (rows, rows), 1)
 
-    def attend(i):
-        here = pl.ds(pl.multiple_of(i * rows, rows), rows)
-        span = pl.ds(pl.multiple_of(i * rows, rows), window)
-        q = q_all[here, :]
-        d = d_all[here, :]
-        k = ext_k[span, :]
-        v = ext_v[span, :]
+    def soften(i, carry):
+        q = q_all[pl.ds(pl.multiple_of(i * rows, rows), rows), :]
+        k = ext_k[pl.ds(pl.multiple_of(i * rows, rows), window), :]
         score = nt_dot(k, q)
-        dprob = nt_dot(v, d)
         mine = blk * n + i
         doc = docs[mine]
         parts = []
@@ -159,8 +149,32 @@
         top = jnp.max(score, axis=0, keepdims=True)
         weight = jnp.exp((score - top) * scale)
         share = 1.0 / jnp.sum(weight, axis=0, keepdims=True)
-        delta = jnp.sum(weight * dprob, axis=0, keepdims=True) * share
-        prob = weight * share
+        prob_all[pl.ds(pl.multiple_of(i * window, window), window), :] = weight * share
+        return carry
+
+    lax.fori_loop(0, n, soften, 0)
+
+    arrived(2)
+
+    @pl.when(blk < groups - 1)
+    def _():
+        forward(ext_v, 1).start()
+
+    arrived(3)
+
+    @pl.when(blk > 0)
+    def _():
+        forward(ext_v, 1).wait_recv()
+
+    def attend(i):
+        here = pl.ds(pl.multiple_of(i * rows, rows), rows)
+        span = pl.ds(pl.multiple_of(i * rows, rows), window)
+        q = q_all[here, :]
+        d = d_all[here, :]
+        k = ext_k[span, :]
+        dprob = nt_dot(ext_v[span, :], d)
+        prob = prob_all[pl.ds(pl.multiple_of(i * window, window), window), :]
+        delta = jnp.sum(prob * dprob, axis=0, keepdims=True)
         dscore = (prob * ((dprob - delta) * scale)).astype(jnp.bfloat16)
         dv_acc[span, :] += nn_dot(prob.astype(jnp.bfloat16), d)
         dk_acc[span, :] += nn_dot(dscore, q)
@@ -223,14 +237,25 @@
     def _():
         handing(give_k, back_k, 0).wait_recv()
         handing(give_v, back_v, 1).wait_recv()
-        dk_acc[pl.ds(tail, far), :] += back_k[...].astype(jnp.float32)
-        dv_acc[pl.ds(tail, far), :] += back_v[...].astype(jnp.float32)
-
-    dk_low[...] = dk_acc[pl.ds(far, n * rows), :].astype(jnp.bfloat16)
-    dv_low[...] = dv_acc[pl.ds(far, n * rows), :].astype(jnp.bfloat16)
+
+    def settle(j):
+        here = pl.ds(pl.multiple_of(j * rows, rows), rows)
+        there = pl.ds(pl.multiple_of(far + j * rows, rows), rows)
+
+        @pl.when((blk < groups - 1) & (j >= n - reach))
+        def _():
+            late = pl.ds(pl.multiple_of((j - (n - reach)) * rows, rows), rows)
+            dk_acc[there, :] += back_k[late, :].astype(jnp.float32)
+            dv_acc[there, :] += back_v[late, :].astype(jnp.float32)
+
+        dk_low[here, :] = dk_acc[there, :].astype(jnp.bfloat16)
+        dv_low[here, :] = dv_acc[there, :].astype(jnp.bfloat16)
+
+    settle(lax.rem(me + 1, n))
 
     def spread(s, carry):
         to = lax.rem(me + s, n)
+        settle(lax.rem(me + s + 1, n))
         give(dk_low, gk, 1, to)
         give(dv_low, gv, 2, to)
         return carry
@@ -257,6 +282,17 @@
     def _():
         handing(give_k, back_k, 0).wait_send()
         handing(give_v, back_v, 1).wait_send()
+
+
+def deliver(a_in, b_in, c_in, a_out, b_out, c_out, sems):
+    copies = [
+        pltpu.make_async_copy(src, dst, sems.at[i])
+        for i, (src, dst) in enumerate(((a_in, a_out), (b_in, b_out), (c_in, c_out)))
+    ]
+    for copy in copies:
+        copy.start()
+    for copy in copies:
+        copy.wait()
 
 
 def body(n, groups, queries, keys, values, grad_out, doc_start):
@@ -267,28 +303,38 @@
     here = (n * rows, width)
     reach = (far + n * rows, width)
     out = jax.ShapeDtypeStruct((rows, total), low)
-    any_space = pl.BlockSpec(memory_space=pl.ANY)
+    hbm = pl.BlockSpec(memory_space=pltpu.HBM)
     vmem = pl.BlockSpec(memory_space=pltpu.VMEM)
     dma = pltpu.SemaphoreType.DMA
-    return pl.pallas_call(
+    grads = pl.pallas_call(
         functools.partial(kernel, n, groups, rows, width),
         out_shape=(out, out, out),
-        in_specs=[pl.BlockSpec(memory_space=pltpu.SMEM)] + [any_space] * 4,
+        in_specs=[hbm] * 5,
         out_specs=(vmem, vmem, vmem),
         scratch_shapes=[
+            pltpu.SMEM(doc_start.shape, jnp.int32),
+            pltpu.VMEM((n * MAXB * rows, rows), wide),
             pltpu.VMEM(reach, low), pltpu.VMEM(reach, low),
             pltpu.VMEM(here, low), pltpu.VMEM(here, low),
             pltpu.VMEM(reach, wide), pltpu.VMEM(reach, wide),
             pltpu.VMEM(here, low), pltpu.VMEM(here, low), pltpu.VMEM(here, low),
             pltpu.VMEM((far, width), low), pltpu.VMEM((far, width), low),
             pltpu.VMEM((far, width), low), pltpu.VMEM((far, width), low),
-            dma((4,)), dma((4,)), dma((4,)), dma((2,)), dma((2,)), dma((2,)), dma((2,)),
+            dma(()), dma((4,)), dma((4,)), dma((4,)),
+            dma((2,)), dma((2,)), dma((2,)), dma((2,)),
             dma((3,)), dma((3,)), dma((3,)),
         ],
         compiler_params=pltpu.CompilerParams(
-            collective_id=0, has_side_effects=True, vmem_limit_bytes=48 * 1024 * 1024
+            collective_id=0, has_side_effects=True, vmem_limit_bytes=36 * 1024 * 1024
         ),
     )(doc_start, queries, keys, values, grad_out)
+    return pl.pallas_call(
+        deliver,
+        out_shape=(out, out, out),
+        in_specs=[vmem] * 3,
+        out_specs=(hbm, hbm, hbm),
+        scratch_shapes=[dma((3,))],
+    )(*grads)
 
 
 def solution(mesh):

time: 102 us -> 103 us (level)
  Pallas kernels: 93.4 us -> 95 us
    pallas_call x0 -> x1, Pallas kernels: none -> 2.52 us  [body(): pl.pallas_call(deliver, out_shape=(out, out, out), in_specs=[vmem] * 3, o...]
    unnamed x13 -> x16, local copies, waits for them, and re-layouts: 7.19 us -> 7.21 us
where the time goes in v1:
time: 103 us
  Pallas kernels  95 us (92%)
  local copies, waits for them, and re-layouts  7.21 us (7%)
    pallas_call x1, Pallas kernels, body(): pl.pallas_call(functools.partial(kernel, n, groups, rows, width), out_sha...  92.5 us
    unnamed x16, local copies, waits for them, and re-layouts  7.21 us
    pallas_call x1, Pallas kernels, body(): pl.pallas_call(deliver, out_shape=(out, out, out), in_specs=[vmem] * 3, o...  2.52 us

profile of v1, /device:TPU:27, one launch (start us, length us, event | category | flops | bytes accessed | tf_op | source)
XLA Modules:
  0.0 102.9 jit_solution(6050758837211033424)
XLA Ops:
  0.6 0.0 copy-start
  0.6 1.0 %copy-done = bf16[128,2048]{1,0:T(8,128)(2,1)S(1)} copy-done((bf16[128,2048]{1,0:T(8,128)(2,1)S(1)}, bf16[128,2048]{1,0:T(8,128)(2,1)}, u32[]{:S(2)}) %copy-start) | copy-done | bytes 524312
  1.7 0.0 copy-start.1
  1.7 1.0 %copy-done.1 = bf16[128,2048]{1,0:T(8,128)(2,1)S(1)} copy-done((bf16[128,2048]{1,0:T(8,128)(2,1)S(1)}, bf16[128,2048]{1,0:T(8,128)(2,1)}, u32[]{:S(2)}) %copy-start.1) | copy-done | bytes 524312
  2.7 0.0 copy-start.2
  2.7 1.0 %copy-done.2 = bf16[128,2048]{1,0:T(8,128)(2,1)S(1)} copy-done((bf16[128,2048]{1,0:T(8,128)(2,1)S(1)}, bf16[128,2048]{1,0:T(8,128)(2,1)}, u32[]{:S(2)}) %copy-start.2) | copy-done | bytes 524312
  3.8 0.0 copy-start.3
  3.8 1.0 %copy-done.3 = bf16[128,2048]{1,0:T(8,128)(2,1)S(1)} copy-done((bf16[128,2048]{1,0:T(8,128)(2,1)S(1)}, bf16[128,2048]{1,0:T(8,128)(2,1)}, u32[]{:S(2)}) %copy-start.3) | copy-done | bytes 524312
  4.8 0.0 copy-start.7
  4.8 0.7 copy-done.7
  5.5 92.5 %shard_map.76 = (bf16[128,2048]{1,0:T(8,128)(2,1)S(1)}, bf16[128,2048]{1,0:T(8,128)(2,1)S(1)}, bf16[128,2048]{1,0:T(8,128)(2,1)S(1)}) custom-call(s32[32]{0:T(128)S(1)} %copy-done.7, bf16[128,2048]{1,0:T(8,128)(2,1)S(1)} %copy-done, bf16[128,2048]{1,0:T(8,128)(2,1)S(1)} %copy-done.1, bf16[128,2048]{1,0:T(8,128)(2,1)S(1)} %copy-done.2, ...), custom_call_target="tpu_custom_call" | custom-call | tf_op jit(solution)/shard_map/pallas_call | solution.py:309
  98.0 0.0 copy-start.4
  98.0 0.8 copy-done.4
  98.8 0.0 copy-start.5
  98.8 0.8 copy-done.5
  99.6 0.0 copy-start.6
  99.6 0.8 copy-done.6
  100.4 2.5 %shard_map.77 = (bf16[128,2048]{1,0:T(8,128)(2,1)}, bf16[128,2048]{1,0:T(8,128)(2,1)}, bf16[128,2048]{1,0:T(8,128)(2,1)}) custom-call(bf16[128,2048]{1,0:T(8,128)(2,1)} %copy-done.4, bf16[128,2048]{1,0:T(8,128)(2,1)} %copy-done.5, bf16[128,2048]{1,0:T(8,128)(2,1)} %copy-done.6), custom_call_target="tpu_custom_call" | custom-call | tf_op jit(solution)/shard_map/pallas_call | solution.py:331
Async XLA Ops:
  0.6 1.0 %copy-start = (bf16[128,2048]{1,0:T(8,128)(2,1)S(1)}, bf16[128,2048]{1,0:T(8,128)(2,1)}, u32[]{:S(2)}) copy-start(bf16[128,2048]{1,0:T(8,128)(2,1)} %q_in.1) | copy-start | bytes 1572868
  1.7 1.0 %copy-start.1 = (bf16[128,2048]{1,0:T(8,128)(2,1)S(1)}, bf16[128,2048]{1,0:T(8,128)(2,1)}, u32[]{:S(2)}) copy-start(bf16[128,2048]{1,0:T(8,128)(2,1)} %k_in.1) | copy-start | bytes 1572868
  2.7 1.0 %copy-start.2 = (bf16[128,2048]{1,0:T(8,128)(2,1)S(1)}, bf16[128,2048]{1,0:T(8,128)(2,1)}, u32[]{:S(2)}) copy-start(bf16[128,2048]{1,0:T(8,128)(2,1)} %v_in.1) | copy-start | bytes 1572868
  3.8 1.0 %copy-start.3 = (bf16[128,2048]{1,0:T(8,128)(2,1)S(1)}, bf16[128,2048]{1,0:T(8,128)(2,1)}, u32[]{:S(2)}) copy-start(bf16[128,2048]{1,0:T(8,128)(2,1)} %d_in.1) | copy-start | bytes 1572868
  4.8 0.7 copy-start.7
  98.0 0.8 copy-start.4
  98.8 0.8 copy-start.5
  99.6 0.8 copy-start.6

commit v2 on v1

--- a/solution.py
+++ b/solution.py
@@ -310,7 +310,7 @@
         functools.partial(kernel, n, groups, rows, width),
         out_shape=(out, out, out),
         in_specs=[hbm] * 5,
-        out_specs=(vmem, vmem, vmem),
+        out_specs=(hbm, hbm, hbm),
         scratch_shapes=[
             pltpu.SMEM(doc_start.shape, jnp.int32),
             pltpu.VMEM((n * MAXB * rows, rows), wide),
@@ -325,7 +325,7 @@
             dma((3,)), dma((3,)), dma((3,)),
         ],
         compiler_params=pltpu.CompilerParams(
-            collective_id=0, has_side_effects=True, vmem_limit_bytes=36 * 1024 * 1024
+            collective_id=0, has_side_effects=True, vmem_limit_bytes=56 * 1024 * 1024
         ),
     )(doc_start, queries, keys, values, grad_out)
     return pl.pallas_call(

time: 103 us -> 96.6 us (0.938)
  local copies, waits for them, and re-layouts: 7.21 us -> 0 us
    unnamed x16 -> x0, local copies, waits for them, and re-layouts: 7.21 us -> none
where the time goes in v2:
time: 96.6 us; the launch traced here: 96.4 us
  Pallas kernels  95.8 us (99%)
    pallas_call x1, Pallas kernels, body(): pl.pallas_call(functools.partial(kernel, n, groups, rows, width), out_sha...  93.3 us
    pallas_call x1, Pallas kernels, body(): pl.pallas_call(deliver, out_shape=(out, out, out), in_specs=[vmem] * 3, o...  2.52 us

profile of v2, /device:TPU:27, one launch (start us, length us, event | category | flops | bytes accessed | tf_op | source)
XLA Modules:
  0.0 96.4 jit_solution(14702053090447875243)
XLA Ops:
  0.6 93.3 %shard_map.76 = (bf16[128,2048]{1,0:T(8,128)(2,1)}, bf16[128,2048]{1,0:T(8,128)(2,1)}, bf16[128,2048]{1,0:T(8,128)(2,1)}) custom-call(s32[32]{0:T(128)} %docs_in.1, bf16[128,2048]{1,0:T(8,128)(2,1)} %q_in.1, bf16[128,2048]{1,0:T(8,128)(2,1)} %k_in.1, bf16[128,2048]{1,0:T(8,128)(2,1)} %v_in.1, bf16[128,2048]{1,0:T(8,128)(2,1)} %d_in.1), custom_call_target="tpu_custom_call" | custom-call | tf_op jit(solution)/shard_map/pallas_call | solution.py:309
  93.9 2.5 %shard_map.77 = (bf16[128,2048]{1,0:T(8,128)(2,1)}, bf16[128,2048]{1,0:T(8,128)(2,1)}, bf16[128,2048]{1,0:T(8,128)(2,1)}) custom-call(bf16[128,2048]{1,0:T(8,128)(2,1)} %get-tuple-element.6.a_in, bf16[128,2048]{1,0:T(8,128)(2,1)} %get-tuple-element.7.b_in, bf16[128,2048]{1,0:T(8,128)(2,1)} %get-tuple-element.8.c_in), custom_call_target="tpu_custom_call" | custom-call | tf_op jit(solution)/shard_map/pallas_call | solution.py:331

commit v3 on v2

--- a/solution.py
+++ b/solution.py
@@ -233,36 +233,35 @@
 
     keep(dq_low, gq, 0).start()
 
-    @pl.when(blk < groups - 1)
-    def _():
-        handing(give_k, back_k, 0).wait_recv()
-        handing(give_v, back_v, 1).wait_recv()
-
-    def settle(j):
-        here = pl.ds(pl.multiple_of(j * rows, rows), rows)
-        there = pl.ds(pl.multiple_of(far + j * rows, rows), rows)
-
-        @pl.when((blk < groups - 1) & (j >= n - reach))
-        def _():
-            late = pl.ds(pl.multiple_of((j - (n - reach)) * rows, rows), rows)
-            dk_acc[there, :] += back_k[late, :].astype(jnp.float32)
-            dv_acc[there, :] += back_v[late, :].astype(jnp.float32)
-
-        dk_low[here, :] = dk_acc[there, :].astype(jnp.bfloat16)
-        dv_low[here, :] = dv_acc[there, :].astype(jnp.bfloat16)
-
-    settle(lax.rem(me + 1, n))
-
-    def spread(s, carry):
-        to = lax.rem(me + s, n)
-        settle(lax.rem(me + s + 1, n))
-        give(dk_low, gk, 1, to)
-        give(dv_low, gv, 2, to)
-        return carry
-
-    lax.fori_loop(1, n, spread, 0)
-    keep(dk_low, gk, 1).start()
-    keep(dv_low, gv, 2).start()
+    for a, acc, low, give_far, back, dst in (
+        (0, dk_acc, dk_low, give_k, back_k, gk),
+        (1, dv_acc, dv_low, give_v, back_v, gv),
+    ):
+        @pl.when(blk < groups - 1)
+        def _(a=a, give_far=give_far, back=back):
+            handing(give_far, back, a).wait_recv()
+
+        def settle(j, acc=acc, low=low, back=back):
+            here = pl.ds(pl.multiple_of(j * rows, rows), rows)
+            there = pl.ds(pl.multiple_of(far + j * rows, rows), rows)
+
+            @pl.when((blk < groups - 1) & (j >= n - reach))
+            def _():
+                late = pl.ds(pl.multiple_of((j - (n - reach)) * rows, rows), rows)
+                acc[there, :] += back[late, :].astype(jnp.float32)
+
+            low[here, :] = acc[there, :].astype(jnp.bfloat16)
+
+        settle(lax.rem(me + 1, n))
+
+        def spread(s, carry, a=a, low=low, dst=dst, settle=settle):
+            to = lax.rem(me + s, n)
+            settle(lax.rem(me + s + 1, n))
+            give(low, dst, a + 1, to)
+            return carry
+
+        lax.fori_loop(1, n, spread, 0)
+        keep(low, dst, a + 1).start()
 
     for a, (src, dst) in enumerate(((dq_low, gq), (dk_low, gk), (dv_low, gv))):
         keep(src, dst, a).wait()
@@ -284,15 +283,23 @@
         handing(give_v, back_v, 1).wait_send()
 
 
-def deliver(a_in, b_in, c_in, a_out, b_out, c_out, sems):
-    copies = [
-        pltpu.make_async_copy(src, dst, sems.at[i])
-        for i, (src, dst) in enumerate(((a_in, a_out), (b_in, b_out), (c_in, c_out)))
-    ]
-    for copy in copies:
-        copy.start()
-    for copy in copies:
-        copy.wait()
+def deliver(a_in, b_in, c_in, a_out, b_out, c_out, held, load_sems, store_sems):
+    parts = load_sems.shape[0] // 3
+    step = held.shape[1] // parts
+    loads, stores = [], []
+    for i, (src, dst) in enumerate(((a_in, a_out), (b_in, b_out), (c_in, c_out))):
+        for c in range(parts):
+            at = pl.ds(c * step, step)
+            mid, sem = held.at[i, at, :], i * parts + c
+            loads.append(pltpu.make_async_copy(src.at[at, :], mid, load_sems.at[sem]))
+            stores.append(pltpu.make_async_copy(mid, dst.at[at, :], store_sems.at[sem]))
+    for load in loads:
+        load.start()
+    for load, store in zip(loads, stores):
+        load.wait()
+        store.start()
+    for store in stores:
+        store.wait()
 
 
 def body(n, groups, queries, keys, values, grad_out, doc_start):
@@ -331,9 +338,10 @@
     return pl.pallas_call(
         deliver,
         out_shape=(out, out, out),
-        in_specs=[vmem] * 3,
+        in_specs=[hbm] * 3,
         out_specs=(hbm, hbm, hbm),
-        scratch_shapes=[dma((3,))],
+        scratch_shapes=[pltpu.VMEM((3, rows, total), low), dma((12,)), dma((12,))],
+        compiler_params=pltpu.CompilerParams(vmem_limit_bytes=56 * 1024 * 1024),
     )(*grads)
 
 

time: 96.6 us -> 93.5 us (0.968)
  Pallas kernels: 95.8 us -> 91.8 us
    pallas_call x1, Pallas kernels: 93.3 us -> 89.5 us  [body(): pl.pallas_call(functools.partial(kernel, n, groups, rows, width), out_sha...]
where the time goes in v3:
time: 93.5 us; the launch traced here: 92.5 us
  Pallas kernels  91.8 us (98%)
    pallas_call x1, Pallas kernels, body(): pl.pallas_call(functools.partial(kernel, n, groups, rows, width), out_sha...  89.5 us
    pallas_call x1, Pallas kernels, body(): pl.pallas_call(deliver, out_shape=(out, out, out), in_specs=[hbm] * 3, ou...  2.33 us

profile of v3, /device:TPU:27, one launch (start us, length us, event | category | flops | bytes accessed | tf_op | source)
XLA Modules:
  0.0 92.5 jit_solution(17711206114076226111)
XLA Ops:
  0.6 89.5 %shard_map.76 = (bf16[128,2048]{1,0:T(8,128)(2,1)}, bf16[128,2048]{1,0:T(8,128)(2,1)}, bf16[128,2048]{1,0:T(8,128)(2,1)}) custom-call(s32[32]{0:T(128)} %docs_in.1, bf16[128,2048]{1,0:T(8,128)(2,1)} %q_in.1, bf16[128,2048]{1,0:T(8,128)(2,1)} %k_in.1, bf16[128,2048]{1,0:T(8,128)(2,1)} %v_in.1, bf16[128,2048]{1,0:T(8,128)(2,1)} %d_in.1), custom_call_target="tpu_custom_call" | custom-call | tf_op jit(solution)/shard_map/pallas_call | solution.py:316
  90.1 2.3 %shard_map.77 = (bf16[128,2048]{1,0:T(8,128)(2,1)}, bf16[128,2048]{1,0:T(8,128)(2,1)}, bf16[128,2048]{1,0:T(8,128)(2,1)}) custom-call(bf16[128,2048]{1,0:T(8,128)(2,1)} %get-tuple-element.6.a_in, bf16[128,2048]{1,0:T(8,128)(2,1)} %get-tuple-element.7.b_in, bf16[128,2048]{1,0:T(8,128)(2,1)} %get-tuple-element.8.c_in), custom_call_target="tpu_custom_call" | custom-call | tf_op jit(solution)/shard_map/pallas_call | solution.py:338

commit v4 on v3

--- a/solution.py
+++ b/solution.py
@@ -30,7 +30,7 @@
     gq, gk, gv,
     docs, prob_all, ext_k, ext_v, q_all, d_all, dk_acc, dv_acc, dq_low, dk_low, dv_low,
     give_k, give_v, back_k, back_v,
-    docs_sem, own_sem, in_send, in_recv, far_send, far_recv, back_send, back_recv,
+    docs_sem, d_recv, own_sem, in_send, in_recv, far_send, far_recv, back_send, back_recv,
     out_own, out_send, out_recv,
 ):
     blk = lax.axis_index("blk")
@@ -82,7 +82,7 @@
                 src_ref=columns(src, to),
                 dst_ref=block(dst, base, me),
                 send_sem=in_send.at[a],
-                recv_sem=in_recv.at[a],
+                recv_sem=d_recv.at[me] if a == 3 else in_recv.at[a],
                 device_id=(blk, to),
                 device_id_type=MESH,
             ).start()
@@ -160,13 +160,20 @@
     def _():
         forward(ext_v, 1).start()
 
-    arrived(3)
-
     @pl.when(blk > 0)
     def _():
         forward(ext_v, 1).wait_recv()
 
     def attend(i):
+        @pl.when(i == me)
+        def _():
+            own[3].wait()
+
+        @pl.when(i != me)
+        def _():
+            landed = block(d_all, 0, i)
+            pltpu.make_async_copy(landed, landed, d_recv.at[i]).wait()
+
         here = pl.ds(pl.multiple_of(i * rows, rows), rows)
         span = pl.ds(pl.multiple_of(i * rows, rows), window)
         q = q_all[here, :]
@@ -196,13 +203,15 @@
         return pltpu.make_async_copy(block(src, 0, me), columns(dst, me), out_own.at[a])
 
     def run(first, count):
+        shift = -(-(first + 1 + count) // count) * count - first - 1
+
         def order(s):
-            return first + lax.rem(me + s, count)
+            return first + lax.rem(me - s + shift, count)
 
         def step(s, carry):
             @pl.when(s > 0)
             def _():
-                give(dq_low, gq, 0, order(s + count - 1))
+                give(dq_low, gq, 0, order(s - 1))
 
             attend(order(s))
             return carry
@@ -327,7 +336,7 @@
             pltpu.VMEM(here, low), pltpu.VMEM(here, low), pltpu.VMEM(here, low),
             pltpu.VMEM((far, width), low), pltpu.VMEM((far, width), low),
             pltpu.VMEM((far, width), low), pltpu.VMEM((far, width), low),
-            dma(()), dma((4,)), dma((4,)), dma((4,)),
+            dma(()), dma((n,)), dma((4,)), dma((4,)), dma((3,)),
             dma((2,)), dma((2,)), dma((2,)), dma((2,)),
             dma((3,)), dma((3,)), dma((3,)),
         ],

time: 93.5 us -> 94.5 us (1.011)
  the two profiles are of different devices: /device:TPU:27 before, /device:TPU:31 now
where the time goes in v4:
time: 94.5 us; the launch traced here: 94.3 us
  Pallas kernels  93.7 us (99%)
    pallas_call x1, Pallas kernels, body(): pl.pallas_call(functools.partial(kernel, n, groups, rows, width), out_sha...  91.3 us
    pallas_call x1, Pallas kernels, body(): pl.pallas_call(deliver, out_shape=(out, out, out), in_specs=[hbm] * 3, ou...  2.33 us

profile of v4, /device:TPU:31, one launch (start us, length us, event | category | flops | bytes accessed | tf_op | source)
XLA Modules:
  0.0 94.3 jit_solution(3899355858347087284)
XLA Ops:
  0.6 91.3 %shard_map.76 = (bf16[128,2048]{1,0:T(8,128)(2,1)}, bf16[128,2048]{1,0:T(8,128)(2,1)}, bf16[128,2048]{1,0:T(8,128)(2,1)}) custom-call(s32[32]{0:T(128)} %docs_in.1, bf16[128,2048]{1,0:T(8,128)(2,1)} %q_in.1, bf16[128,2048]{1,0:T(8,128)(2,1)} %k_in.1, bf16[128,2048]{1,0:T(8,128)(2,1)} %v_in.1, bf16[128,2048]{1,0:T(8,128)(2,1)} %d_in.1), custom_call_target="tpu_custom_call" | custom-call | tf_op jit(solution)/shard_map/pallas_call | solution.py:325
  92.0 2.3 %shard_map.77 = (bf16[128,2048]{1,0:T(8,128)(2,1)}, bf16[128,2048]{1,0:T(8,128)(2,1)}, bf16[128,2048]{1,0:T(8,128)(2,1)}) custom-call(bf16[128,2048]{1,0:T(8,128)(2,1)} %get-tuple-element.6.a_in, bf16[128,2048]{1,0:T(8,128)(2,1)} %get-tuple-element.7.b_in, bf16[128,2048]{1,0:T(8,128)(2,1)} %get-tuple-element.8.c_in), custom_call_target="tpu_custom_call" | custom-call | tf_op jit(solution)/shard_map/pallas_call | solution.py:347
